TPU v7x, 256 devices: a whole 4x4x8 slice. The times are simulated.
256 devices in a mesh: row: 16 (over y, x), col: 16 (over z, core).
Axes of the slice: x: 4, y: 4, z: 8, core: 2. Of those that a mesh axis runs over, the one named last changes fastest.
Arguments:
- diag_inv: float32 [2, 2048, 2048], P(None, 'col', 'row'), may hold values from -0.125 to 0.125
- cross_block: float32 [2048, 2048], P('row', 'col'), may hold values from -0.125 to 0.125
- coupling: float32 [2, 2048, 65536], P(None, 'row', 'col'), may hold values from -0.125 to 0.125
- panel_loads: float32 [2, 1024, 2048], P(None, 'row', 'col'), may hold values from -6 to 6
- rest_loads: float32 [1024, 65536], P('row', 'col'), may hold values from -6 to 6
Outputs:
- solved: float32 [2, 1024, 2048], P(None, None, 'row')
- rest_updated: float32 [1024, 65536], P('row', 'col')
All inputs are finite; a program needn't handle non-finite values.
Results may differ from a plain program's by a relative error of at most 0.00008.
Values sent between devices are 32-bit elements; how exact they have to be, the bound alone decides.
A program may use at most 128 MiB of HBM per device.

v0:
```python
import jax
import jax.numpy as jnp
from jax import lax
from jax.sharding import PartitionSpec as P


def product(left, right):
    return jnp.dot(left, right, precision=lax.Precision.HIGHEST, preferred_element_type=jnp.float32)


def local(diag_inv, cross_block, coupling, panel_loads, rest_loads):
    both_full = lax.all_gather(panel_loads, "row", axis=1, tiled=True)

    def solve_panel(loads_full, panel_index):
        partial_value = product(loads_full, diag_inv[panel_index])
        return lax.psum(partial_value, "col")

    upper_solved = solve_panel(both_full[1], 1)
    lower_local = panel_loads[0] - lax.psum_scatter(
        product(upper_solved, cross_block), "row", scatter_dimension=0, tiled=True
    )
    lower_full = lax.all_gather(lower_local, "row", axis=0, tiled=True)
    lower_solved = solve_panel(lower_full, 0)

    def apply_panel(current, solved_part, panel_index):
        return current - lax.psum_scatter(
            product(solved_part, coupling[panel_index]), "row", scatter_dimension=0, tiled=True
        )

    rest_updated = apply_panel(rest_loads, upper_solved, 1)
    rest_updated = apply_panel(rest_updated, lower_solved, 0)
    return (jnp.stack([lower_solved, upper_solved]), rest_updated)


def solution(mesh):
    in_specs = (
        P(None, "col", "row"),
        P("row", "col"),
        P(None, "row", "col"),
        P(None, "row", "col"),
        P("row", "col"),
    )
    out_specs = (P(None, None, "row"), P("row", "col"))
    return jax.shard_map(local, mesh=mesh, in_specs=in_specs, out_specs=out_specs, check_vma=False)
```

profile of v0, /device:TPU:1, one launch (start us, length us, event | category | flops | bytes accessed | tf_op | source)
XLA Modules:
  0.0 639.2 jit_solution(14545961122653395243)
XLA Ops:
  7.2 0.0 copy-start
  7.2 0.0 all-gather.2.cloned.1.call-start
  7.2 0.7 all-gather.2.cloned.1.call-update
  7.9 0.0 all-reduce.3.cloned.1.call-start
  8.0 52.6 %all-gather.2.cloned.1.call-done = f32[2,1024,128]{2,1,0:T(8,128)} async-done(((f32[2,64,128]{2,1,0:T(8,128)}), f32[2,1024,128]{2,1,0:T(8,128)}) %all-gather.2.cloned.1.call-update) | async-done | bytes 1048592 | tf_op jit(solution)/shard_map/all_gather | solution.py:12
  60.6 2.4 fusion.6
  63.0 0.0 all-reduce.3.cloned.1.call-update
  63.0 0.0 reduce-scatter.4.cloned.1.call-start
  63.0 110.8 %all-reduce.3.cloned.1.call-done = f32[1024,128]{1,0:T(8,128)} async-done(((f32[1024,128]{1,0:T(8,128)}), f32[1024,128]{1,0:T(8,128)}) %all-reduce.3.cloned.1.call-update) | async-done | bytes 524304 | tf_op jit(solution)/shard_map/psum | solution.py:16
  173.8 0.0 copy-done
  173.8 0.0 copy-start.1
  173.8 2.5 fusion.12
  176.3 0.0 reduce-scatter.4.cloned.1.call-update
  176.3 0.0 all-reduce.5.cloned.1.call-start
  176.4 78.0 %reduce-scatter.4.cloned.1.call-done = f32[64,128]{1,0:T(8,128)} async-done(((f32[1024,128]{1,0:T(8,128)}), f32[64,128]{1,0:T(8,128)}) %reduce-scatter.4.cloned.1.call-update) | async-done | bytes 32784 | tf_op jit(solution)/shard_map/reduce_scatter | solution.py:19
  254.3 0.8 bitcast_subtract_fusion
  255.1 17.5 %all_gather.7 = f32[1024,128]{1,0:T(8,128)S(1)} all-gather(f32[64,128]{1,0:T(8,128)S(1)} %bitcast_subtract_fusion), channel_id=1, replica_groups=mesh['row'=16,'col'=16] {'row'}, dimensions={0}, use_global_device_ids=true | all-gather | bytes 557056 | tf_op jit(solution)/shard_map/all_gather | solution.py:22
  272.6 2.2 fusion.7
  274.8 0.0 all-reduce.5.cloned.1.call-update
  274.8 0.0 reduce-scatter.6.cloned.1.call-start
  274.9 0.0 copy-done.1
  274.9 16.7 %fusion.2 = f32[1024,4096]{1,0:T(8,128)} fusion(f32[1024,128]{1,0:T(8,128)S(1)} %copy-done.1, f32[2,128,4096]{2,1,0:T(8,128)} %param.7), kind=kOutput, calls=%fused_computation.2 | convolution fusion | flops 6442450944 | bytes 19398656 | tf_op jit(solution)/shard_map/dot_general | solution.py:8
  291.6 0.0 reduce-scatter.6.cloned.1.call-update
  291.6 0.0 reduce-scatter.8.cloned.1.call-start
  291.7 99.1 %all-reduce.5.cloned.1.call-done = f32[1024,128]{1,0:T(8,128)} async-done(((f32[1024,128]{1,0:T(8,128)}), f32[1024,128]{1,0:T(8,128)}) %all-reduce.5.cloned.1.call-update) | async-done | bytes 524304 | tf_op jit(solution)/shard_map/psum | solution.py:16
  390.8 17.1 %fusion = f32[1024,4096]{1,0:T(8,128)} fusion(f32[1024,128]{1,0:T(8,128)} %all-reduce.5.cloned.1.call-done, f32[2,128,4096]{2,1,0:T(8,128)} %param.7), kind=kOutput, calls=%fused_computation | convolution fusion | flops 6442450944 | bytes 19398656 | tf_op jit(solution)/shard_map/dot_general | solution.py:8
  407.9 0.0 copy-start.2
  407.9 0.0 copy-start.3
  407.9 0.0 reduce-scatter.8.cloned.1.call-update
  407.9 1.0 copy-done.2
  408.9 1.0 pad_maximum_fusion
  410.0 100.4 %reduce-scatter.6.cloned.1.call-done = f32[64,4096]{1,0:T(8,128)} async-done(((f32[1024,4096]{1,0:T(8,128)}), f32[64,4096]{1,0:T(8,128)}) %reduce-scatter.6.cloned.1.call-update) | async-done | bytes 1048592 | tf_op jit(solution)/shard_map/reduce_scatter | solution.py:26
  510.4 119.3 %reduce-scatter.8.cloned.1.call-done = f32[64,4096]{1,0:T(8,128)} async-done(((f32[1024,4096]{1,0:T(8,128)}), f32[64,4096]{1,0:T(8,128)}) %reduce-scatter.8.cloned.1.call-update) | async-done | bytes 1048592 | tf_op jit(solution)/shard_map/reduce_scatter | solution.py:26
  629.7 0.0 copy-done.3
  629.7 2.7 subtract_subtract_fusion
Async XLA Ops:
  7.2 166.6 %copy-start = (f32[128,128]{1,0:T(8,128)S(1)}, f32[128,128]{1,0:T(8,128)}, u32[]{:S(2)}) copy-start(f32[128,128]{1,0:T(8,128)} %param.6) | copy-start | bytes 196612
  7.2 53.4 %all-gather.2.cloned.1.call-start = ((), (), s32[]{:S(2)}) async-start(), calls=%async_computation.3 | async-start | bytes 1114112 | tf_op jit(solution)/shard_map/all_gather | solution.py:12
  7.9 165.9 %all-reduce.3.cloned.1.call-start = ((), (), s32[]{:S(2)}) async-start(), calls=%async_computation.4 | async-start | bytes 1048576 | tf_op jit(solution)/shard_map/psum | solution.py:16
  63.0 191.3 %reduce-scatter.4.cloned.1.call-start = ((), (), s32[]{:S(2)}) async-start(), calls=%async_computation.5 | async-start | bytes 557056 | tf_op jit(solution)/shard_map/reduce_scatter | solution.py:19
  173.8 101.1 %copy-start.1 = (f32[1024,128]{1,0:T(8,128)S(1)}, f32[1024,128]{1,0:T(8,128)}, u32[]{:S(2)}) copy-start(f32[1024,128]{1,0:T(8,128)} %all-reduce.3.cloned.1.call-done) | copy-start | bytes 1572868
  176.3 214.5 %all-reduce.5.cloned.1.call-start = ((), (), s32[]{:S(2)}) async-start(), calls=%async_computation.6 | async-start | bytes 1048576 | tf_op jit(solution)/shard_map/psum | solution.py:16
  274.8 235.6 %reduce-scatter.6.cloned.1.call-start = ((), (), s32[]{:S(2)}) async-start(), calls=%async_computation.7 | async-start | bytes 17825792 | tf_op jit(solution)/shard_map/reduce_scatter | solution.py:26
  291.6 338.1 %reduce-scatter.8.cloned.1.call-start = ((), (), s32[]{:S(2)}) async-start(), calls=%async_computation.8 | async-start | bytes 17825792 | tf_op jit(solution)/shard_map/reduce_scatter | solution.py:26
  407.9 1.1 copy-start.2
  407.9 221.9 %copy-start.3 = (f32[64,4096]{1,0:T(8,128)S(1)}, f32[64,4096]{1,0:T(8,128)}, u32[]{:S(2)}) copy-start(f32[64,4096]{1,0:T(8,128)} %param.9) | copy-start | bytes 3145732
Sparse Core Ops, SparseCore 0:
  10.5 50.0 all-gather.1
  63.5 110.3 all-reduce.2
  178.3 76.0 reduce-scatter.3
  274.9 115.7 all-reduce.4
  394.8 115.5 reduce-scatter.5
  514.4 115.2 reduce-scatter.7
where the time goes:
time: 640 us; the launch traced here: 639 us
  waiting for transfers between devices  561 us (88%)
  matrix products  40.9 us (6%)
  blocking collectives  17.5 us (3%)
  between operations  14.1 us (2%)
    reduce_scatter x2, waiting for transfers between devices, apply_panel(): lax.psum_scatter(product(solved_part, coupling[panel_index]), 'row', scat...  220 us
    psum x2, waiting for transfers between devices, solve_panel(): return lax.psum(partial_value, 'col')  210 us
    reduce_scatter x1, waiting for transfers between devices, local(): lax.psum_scatter(product(upper_solved, cross_block), 'row', scatter_dimen...  78 us
    all_gather x1, waiting for transfers between devices, local(): both_full = lax.all_gather(panel_loads, 'row', axis=1, tiled=True)  52.6 us
    dot_general x5, matrix products, product(): jnp.dot(left, right, precision=lax.Precision.HIGHEST, preferred_element_t...  40.9 us
    all_gather x1, blocking collectives, local(): lower_full = lax.all_gather(lower_local, 'row', axis=0, tiled=True)  17.5 us
  transfers between devices with their start and end apart: 6, of which 6 were waited for; matrix products, arithmetic and copies ran while one was open for 5% of the time, Pallas kernels for 0%

commit v1 on v0

--- a/solution.py
+++ b/solution.py
@@ -9,7 +9,9 @@
 
 
 def local(diag_inv, cross_block, coupling, panel_loads, rest_loads):
-    both_full = lax.all_gather(panel_loads, "row", axis=1, tiled=True)
+    both_full = jnp.concatenate(
+        lax.all_to_all(jnp.stack([panel_loads] * lax.axis_size("row")), "row", 0, 0), axis=1
+    )
 
     def solve_panel(loads_full, panel_index):
         partial_value = product(loads_full, diag_inv[panel_index])

time: 640 us -> 608 us (0.950)
  waiting for transfers between devices: 561 us -> 507 us
  blocking collectives: 17.5 us -> 41 us
    all_gather x1 -> x0, waiting for transfers between devices: 52.6 us -> none  [local(): both_full = lax.all_gather(panel_loads, 'row', axis=1, tiled=True)]
    all_to_all x0 -> x1, blocking collectives: none -> 23.5 us  [local(): lax.all_to_all(jnp.stack([panel_loads] * lax.axis_size('row')), 'row', 0, 0)]
  transfers between devices with their start and end apart: 6 -> 5, of which waited for: 6 -> 5; matrix products, arithmetic and copies ran while one was open for 5% -> 6% of each run, Pallas kernels for 0% -> 0%
where the time goes in v1:
time: 608 us
  waiting for transfers between devices  507 us (83%)
  blocking collectives  41 us (7%)
  matrix products  39.1 us (6%)
  between operations  13.8 us (2%)
    reduce_scatter x2, waiting for transfers between devices, apply_panel(): lax.psum_scatter(product(solved_part, coupling[panel_index]), 'row', scat...  220 us
    psum x2, waiting for transfers between devices, solve_panel(): return lax.psum(partial_value, 'col')  209 us
    reduce_scatter x1, waiting for transfers between devices, local(): lax.psum_scatter(product(upper_solved, cross_block), 'row', scatter_dimen...  78 us
    dot_general x5, matrix products, product(): jnp.dot(left, right, precision=lax.Precision.HIGHEST, preferred_element_t...  39.1 us
    all_to_all x1, blocking collectives, local(): lax.all_to_all(jnp.stack([panel_loads] * lax.axis_size('row')), 'row', 0, 0)  23.5 us
    all_gather x1, blocking collectives, local(): lower_full = lax.all_gather(lower_local, 'row', axis=0, tiled=True)  17.5 us
  transfers between devices with their start and end apart: 5, of which 5 were waited for; matrix products, arithmetic and copies ran while one was open for 6% of the time, Pallas kernels for 0%

profile of v1, /device:TPU:1, one launch (start us, length us, event | category | flops | bytes accessed | tf_op | source)
XLA Modules:
  0.0 607.6 jit_solution(8894372876168847287)
XLA Ops:
  7.2 0.0 copy-start
  7.2 0.0 copy-start.4
  7.2 0.0 copy-start.5
  7.2 0.0 all-reduce.3.cloned.1.call-start
  7.2 1.0 stack.8
  8.2 23.5 %all_to_all.5 = f32[16,2,64,128]{3,2,1,0:T(8,128)S(1)} all-to-all(f32[16,2,64,128]{3,2,1,0:T(8,128)S(1)} %stack.8), channel_id=1, replica_groups=mesh['row'=16,'col'=16] {'row'}, dimensions={0} | all-to-all | bytes 2097152 | tf_op jit(solution)/shard_map/all_to_all | solution.py:13
  31.8 0.0 copy-done.5
  31.8 1.4 fusion.8
  33.2 0.0 all-reduce.3.cloned.1.call-update
  33.2 0.0 reduce-scatter.4.cloned.1.call-start
  33.2 110.1 %all-reduce.3.cloned.1.call-done = f32[1024,128]{1,0:T(8,128)} async-done(((f32[1024,128]{1,0:T(8,128)}), f32[1024,128]{1,0:T(8,128)}) %all-reduce.3.cloned.1.call-update) | async-done | bytes 524304 | tf_op jit(solution)/shard_map/psum | solution.py:18
  143.3 0.0 copy-done
  143.3 0.0 copy-start.1
  143.3 2.5 fusion.12
  145.8 0.0 reduce-scatter.4.cloned.1.call-update
  145.8 0.0 all-reduce.5.cloned.1.call-start
  145.9 78.0 %reduce-scatter.4.cloned.1.call-done = f32[64,128]{1,0:T(8,128)} async-done(((f32[1024,128]{1,0:T(8,128)}), f32[64,128]{1,0:T(8,128)}) %reduce-scatter.4.cloned.1.call-update) | async-done | bytes 32784 | tf_op jit(solution)/shard_map/reduce_scatter | solution.py:21
  223.8 0.0 copy-done.4
  223.8 0.8 bitcast_subtract_fusion
  224.6 17.5 %all_gather.3 = f32[1024,128]{1,0:T(8,128)S(1)} all-gather(f32[64,128]{1,0:T(8,128)S(1)} %bitcast_subtract_fusion), channel_id=1, replica_groups=mesh['row'=16,'col'=16] {'row'}, dimensions={0}, use_global_device_ids=true | all-gather | bytes 557056 | tf_op jit(solution)/shard_map/all_gather | solution.py:24
  242.1 1.4 fusion.6
  243.5 0.0 all-reduce.5.cloned.1.call-update
  243.5 0.0 reduce-scatter.6.cloned.1.call-start
  243.5 0.0 copy-done.1
  243.5 16.8 %fusion.2 = f32[1024,4096]{1,0:T(8,128)} fusion(f32[1024,128]{1,0:T(8,128)S(1)} %copy-done.1, f32[2,128,4096]{2,1,0:T(8,128)} %param.7), kind=kOutput, calls=%fused_computation.2 | convolution fusion | flops 6442450944 | bytes 19398656 | tf_op jit(solution)/shard_map/dot_general | solution.py:8
  260.3 0.0 reduce-scatter.6.cloned.1.call-update
  260.3 0.0 reduce-scatter.8.cloned.1.call-start
  260.4 99.1 %all-reduce.5.cloned.1.call-done = f32[1024,128]{1,0:T(8,128)} async-done(((f32[1024,128]{1,0:T(8,128)}), f32[1024,128]{1,0:T(8,128)}) %all-reduce.5.cloned.1.call-update) | async-done | bytes 524304 | tf_op jit(solution)/shard_map/psum | solution.py:18
  359.4 17.1 %fusion = f32[1024,4096]{1,0:T(8,128)} fusion(f32[1024,128]{1,0:T(8,128)} %all-reduce.5.cloned.1.call-done, f32[2,128,4096]{2,1,0:T(8,128)} %param.7), kind=kOutput, calls=%fused_computation | convolution fusion | flops 6442450944 | bytes 19398656 | tf_op jit(solution)/shard_map/dot_general | solution.py:8
  376.5 0.0 copy-start.2
  376.5 0.0 copy-start.3
  376.5 0.0 reduce-scatter.8.cloned.1.call-update
  376.6 1.0 copy-done.2
  377.6 1.0 pad_maximum_fusion
  378.6 100.4 %reduce-scatter.6.cloned.1.call-done = f32[64,4096]{1,0:T(8,128)} async-done(((f32[1024,4096]{1,0:T(8,128)}), f32[64,4096]{1,0:T(8,128)}) %reduce-scatter.6.cloned.1.call-update) | async-done | bytes 1048592 | tf_op jit(solution)/shard_map/reduce_scatter | solution.py:28
  479.1 119.3 %reduce-scatter.8.cloned.1.call-done = f32[64,4096]{1,0:T(8,128)} async-done(((f32[1024,4096]{1,0:T(8,128)}), f32[64,4096]{1,0:T(8,128)}) %reduce-scatter.8.cloned.1.call-update) | async-done | bytes 1048592 | tf_op jit(solution)/shard_map/reduce_scatter | solution.py:28
  598.4 0.0 copy-done.3
  598.4 2.7 subtract_subtract_fusion
  (1 shorter events, 0.0 us)
Async XLA Ops:
  7.2 136.2 %copy-start = (f32[128,128]{1,0:T(8,128)S(1)}, f32[128,128]{1,0:T(8,128)}, u32[]{:S(2)}) copy-start(f32[128,128]{1,0:T(8,128)} %param.6) | copy-start | bytes 196612
  7.2 216.7 %copy-start.4 = (f32[2,64,128]{2,1,0:T(8,128)S(1)}, f32[2,64,128]{2,1,0:T(8,128)}, u32[]{:S(2)}) copy-start(f32[2,64,128]{2,1,0:T(8,128)} %param.8) | copy-start | bytes 196612
  7.2 24.6 %copy-start.5 = (f32[2,128,128]{2,1,0:T(8,128)S(1)}, f32[2,128,128]{2,1,0:T(8,128)}, u32[]{:S(2)}) copy-start(f32[2,128,128]{2,1,0:T(8,128)} %param.5) | copy-start | bytes 393220
  7.2 136.1 %all-reduce.3.cloned.1.call-start = ((), (), s32[]{:S(2)}) async-start(), calls=%async_computation.4 | async-start | bytes 1048576 | tf_op jit(solution)/shard_map/psum | solution.py:18
  33.2 190.6 %reduce-scatter.4.cloned.1.call-start = ((), (), s32[]{:S(2)}) async-start(), calls=%async_computation.5 | async-start | bytes 557056 | tf_op jit(solution)/shard_map/reduce_scatter | solution.py:21
  143.3 100.2 %copy-start.1 = (f32[1024,128]{1,0:T(8,128)S(1)}, f32[1024,128]{1,0:T(8,128)}, u32[]{:S(2)}) copy-start(f32[1024,128]{1,0:T(8,128)} %all-reduce.3.cloned.1.call-done) | copy-start | bytes 1572868
  145.8 213.6 %all-reduce.5.cloned.1.call-start = ((), (), s32[]{:S(2)}) async-start(), calls=%async_computation.6 | async-start | bytes 1048576 | tf_op jit(solution)/shard_map/psum | solution.py:18
  243.5 235.6 %reduce-scatter.6.cloned.1.call-start = ((), (), s32[]{:S(2)}) async-start(), calls=%async_computation.7 | async-start | bytes 17825792 | tf_op jit(solution)/shard_map/reduce_scatter | solution.py:28
  260.3 338.1 %reduce-scatter.8.cloned.1.call-start = ((), (), s32[]{:S(2)}) async-start(), calls=%async_computation.8 | async-start | bytes 17825792 | tf_op jit(solution)/shard_map/reduce_scatter | solution.py:28
  376.5 1.1 copy-start.2
  376.5 221.9 %copy-start.3 = (f32[64,4096]{1,0:T(8,128)S(1)}, f32[64,4096]{1,0:T(8,128)}, u32[]{:S(2)}) copy-start(f32[64,4096]{1,0:T(8,128)} %param.9) | copy-start | bytes 3145732
Sparse Core Ops, SparseCore 0:
  33.3 109.9 all-reduce.2
  147.8 76.0 reduce-scatter.3
  243.6 115.7 all-reduce.4
  363.4 115.5 reduce-scatter.5
  483.1 115.2 reduce-scatter.7

commit v2 on v0

--- a/solution.py
+++ b/solution.py
@@ -13,7 +13,7 @@
 
     def solve_panel(loads_full, panel_index):
         partial_value = product(loads_full, diag_inv[panel_index])
-        return lax.psum(partial_value, "col")
+        return jnp.sum(lax.all_gather(partial_value, "col"), axis=0)
 
     upper_solved = solve_panel(both_full[1], 1)
     lower_local = panel_loads[0] - lax.psum_scatter(

time: 640 us -> 528 us (0.82)
  waiting for transfers between devices: 561 us -> 445 us
  other arithmetic: 4.48 us -> 12.2 us
    psum x2 -> x0, waiting for transfers between devices: 210 us -> none  [solve_panel(): return lax.psum(partial_value, 'col')]
    all_gather x0 -> x2, waiting for transfers between devices: none -> 103 us  [solve_panel(): return jnp.sum(lax.all_gather(partial_value, 'col'), axis=0)]
    reduce_sum x0 -> x2, other arithmetic: none -> 7.69 us  [solve_panel(): return jnp.sum(lax.all_gather(partial_value, 'col'), axis=0)]
  transfers between devices with their start and end apart: 6 -> 6, of which waited for: 6 -> 6; matrix products, arithmetic and copies ran while one was open for 5% -> 7% of each run, Pallas kernels for 0% -> 0%
where the time goes in v2:
time: 528 us
  waiting for transfers between devices  445 us (84%)
  matrix products  38.6 us (7%)
  blocking collectives  17.5 us (3%)
  between operations  14.1 us (3%)
  other arithmetic  12.2 us (2%)
    reduce_scatter x2, waiting for transfers between devices, apply_panel(): lax.psum_scatter(product(solved_part, coupling[panel_index]), 'row', scat...  215 us
    all_gather x2, waiting for transfers between devices, solve_panel(): return jnp.sum(lax.all_gather(partial_value, 'col'), axis=0)  103 us
    reduce_scatter x1, waiting for transfers between devices, local(): lax.psum_scatter(product(upper_solved, cross_block), 'row', scatter_dimen...  73.9 us
    all_gather x1, waiting for transfers between devices, local(): both_full = lax.all_gather(panel_loads, 'row', axis=1, tiled=True)  52.6 us
    dot_general x5, matrix products, product(): jnp.dot(left, right, precision=lax.Precision.HIGHEST, preferred_element_t...  38.6 us
    all_gather x1, blocking collectives, local(): lower_full = lax.all_gather(lower_local, 'row', axis=0, tiled=True)  17.5 us
  transfers between devices with their start and end apart: 6, of which 6 were waited for; matrix products, arithmetic and copies ran while one was open for 7% of the time, Pallas kernels for 0%

profile of v2, /device:TPU:1, one launch (start us, length us, event | category | flops | bytes accessed | tf_op | source)
XLA Modules:
  0.0 528.0 jit_solution(8853954667262091860)
XLA Ops:
  7.2 0.0 copy-start
  7.2 0.0 all-gather.6.cloned.1.call-start
  7.2 0.7 all-gather.6.cloned.1.call-update
  7.9 0.0 all-gather.8.cloned.1.call-start
  8.0 52.6 %all-gather.6.cloned.1.call-done = f32[2,1024,128]{2,1,0:T(8,128)} async-done(((f32[2,64,128]{2,1,0:T(8,128)}), f32[2,1024,128]{2,1,0:T(8,128)}) %all-gather.6.cloned.1.call-update) | async-done | bytes 1048592 | tf_op jit(solution)/shard_map/all_gather | solution.py:12
  60.6 2.4 fusion.6
  63.0 0.0 all-gather.8.cloned.1.call-update
  63.0 0.0 reduce-scatter.4.cloned.1.call-start
  63.0 57.2 %all-gather.8.cloned.1.call-done = f32[16384,128]{1,0:T(8,128)} async-done(((f32[1024,128]{1,0:T(8,128)}), f32[16384,128]{1,0:T(8,128)}) %all-gather.8.cloned.1.call-update) | async-done | bytes 8388624 | tf_op jit(solution)/shard_map/all_gather | solution.py:16
  120.2 0.0 copy-start.2
  120.2 0.0 copy-start.3
  120.2 3.9 reduce_sum.18
  124.1 0.0 copy-done
  124.1 1.4 fusion.12
  125.5 0.0 reduce-scatter.4.cloned.1.call-update
  125.5 0.0 all-gather.10.cloned.1.call-start
  125.5 73.9 %reduce-scatter.4.cloned.1.call-done = f32[64,128]{1,0:T(8,128)} async-done(((f32[1024,128]{1,0:T(8,128)}), f32[64,128]{1,0:T(8,128)}) %reduce-scatter.4.cloned.1.call-update) | async-done | bytes 32784 | tf_op jit(solution)/shard_map/reduce_scatter | solution.py:19
  199.4 0.0 copy-done.2
  199.4 0.8 bitcast_subtract_fusion
  200.2 17.5 %all_gather.21 = f32[1024,128]{1,0:T(8,128)S(1)} all-gather(f32[64,128]{1,0:T(8,128)S(1)} %bitcast_subtract_fusion), channel_id=1, replica_groups=mesh['row'=16,'col'=16] {'row'}, dimensions={0}, use_global_device_ids=true | all-gather | bytes 557056 | tf_op jit(solution)/shard_map/all_gather | solution.py:22
  217.7 0.0 copy-done.3
  217.7 1.4 fusion.7
  219.0 0.0 all-gather.10.cloned.1.call-update
  219.1 0.0 reduce-scatter.6.cloned.1.call-start
  219.1 16.7 %fusion.2 = f32[1024,4096]{1,0:T(8,128)} fusion(f32[1024,128]{1,0:T(8,128)S(1)} %reduce_sum.18, f32[2,128,4096]{2,1,0:T(8,128)} %param.7), kind=kOutput, calls=%fused_computation.2 | convolution fusion | flops 6442450944 | bytes 19398656 | tf_op jit(solution)/shard_map/dot_general | solution.py:8
  235.9 0.0 reduce-scatter.6.cloned.1.call-update
  235.9 0.0 reduce-scatter.8.cloned.1.call-start
  235.9 45.8 %all-gather.10.cloned.1.call-done = f32[16384,128]{1,0:T(8,128)} async-done(((f32[1024,128]{1,0:T(8,128)}), f32[16384,128]{1,0:T(8,128)}) %all-gather.10.cloned.1.call-update) | async-done | bytes 8388624 | tf_op jit(solution)/shard_map/all_gather | solution.py:16
  281.8 3.8 reduce_sum.19
  285.6 16.7 %fusion = f32[1024,4096]{1,0:T(8,128)} fusion(f32[1024,128]{1,0:T(8,128)S(1)} %reduce_sum.19, f32[2,128,4096]{2,1,0:T(8,128)} %param.7), kind=kOutput, calls=%fused_computation | convolution fusion | flops 6442450944 | bytes 19398656 | tf_op jit(solution)/shard_map/dot_general | solution.py:8
  302.3 0.0 copy-start.1
  302.3 0.0 reduce-scatter.8.cloned.1.call-update
  302.3 1.0 pad_maximum_fusion
  303.4 95.8 %reduce-scatter.6.cloned.1.call-done = f32[64,4096]{1,0:T(8,128)} async-done(((f32[1024,4096]{1,0:T(8,128)}), f32[64,4096]{1,0:T(8,128)}) %reduce-scatter.6.cloned.1.call-update) | async-done | bytes 1048592 | tf_op jit(solution)/shard_map/reduce_scatter | solution.py:26
  399.2 119.4 %reduce-scatter.8.cloned.1.call-done = f32[64,4096]{1,0:T(8,128)} async-done(((f32[1024,4096]{1,0:T(8,128)}), f32[64,4096]{1,0:T(8,128)}) %reduce-scatter.8.cloned.1.call-update) | async-done | bytes 1048592 | tf_op jit(solution)/shard_map/reduce_scatter | solution.py:26
  518.5 0.0 copy-done.1
  518.5 2.7 subtract_subtract_fusion
Async XLA Ops:
  7.2 116.9 %copy-start = (f32[128,128]{1,0:T(8,128)S(1)}, f32[128,128]{1,0:T(8,128)}, u32[]{:S(2)}) copy-start(f32[128,128]{1,0:T(8,128)} %param.6) | copy-start | bytes 196612
  7.2 53.4 %all-gather.6.cloned.1.call-start = ((), (), s32[]{:S(2)}) async-start(), calls=%async_computation.3 | async-start | bytes 1114112 | tf_op jit(solution)/shard_map/all_gather | solution.py:12
  7.9 112.3 %all-gather.8.cloned.1.call-start = ((), (), s32[]{:S(2)}) async-start(), calls=%async_computation.7 | async-start | bytes 8912896 | tf_op jit(solution)/shard_map/all_gather | solution.py:16
  63.0 136.4 %reduce-scatter.4.cloned.1.call-start = ((), (), s32[]{:S(2)}) async-start(), calls=%async_computation.4 | async-start | bytes 557056 | tf_op jit(solution)/shard_map/reduce_scatter | solution.py:19
  120.2 79.2 %copy-start.2 = (f32[2,64,128]{2,1,0:T(8,128)S(1)}, f32[2,64,128]{2,1,0:T(8,128)}, u32[]{:S(2)}) copy-start(f32[2,64,128]{2,1,0:T(8,128)} %param.8) | copy-start | bytes 196612
  120.2 97.5 %copy-start.3 = (f32[2,128,128]{2,1,0:T(8,128)S(1)}, f32[2,128,128]{2,1,0:T(8,128)}, u32[]{:S(2)}) copy-start(f32[2,128,128]{2,1,0:T(8,128)} %param.5) | copy-start | bytes 393220
  125.5 156.3 %all-gather.10.cloned.1.call-start = ((), (), s32[]{:S(2)}) async-start(), calls=%async_computation.8 | async-start | bytes 8912896 | tf_op jit(solution)/shard_map/all_gather | solution.py:16
  219.1 180.1 %reduce-scatter.6.cloned.1.call-start = ((), (), s32[]{:S(2)}) async-start(), calls=%async_computation.5 | async-start | bytes 17825792 | tf_op jit(solution)/shard_map/reduce_scatter | solution.py:26
  235.9 282.6 %reduce-scatter.8.cloned.1.call-start = ((), (), s32[]{:S(2)}) async-start(), calls=%async_computation.6 | async-start | bytes 17825792 | tf_op jit(solution)/shard_map/reduce_scatter | solution.py:26
  302.3 216.2 %copy-start.1 = (f32[64,4096]{1,0:T(8,128)S(1)}, f32[64,4096]{1,0:T(8,128)}, u32[]{:S(2)}) copy-start(f32[64,4096]{1,0:T(8,128)} %param.9) | copy-start | bytes 3145732
Sparse Core Ops, SparseCore 0:
  10.5 50.0 all-gather.5
  63.1 57.0 all-gather.7
  125.6 73.7 reduce-scatter.3
  219.2 62.5 all-gather.9
  285.7 113.3 reduce-scatter.5
  403.2 115.3 reduce-scatter.7
